TPU v7x, 128 devices: a whole 4x4x4 slice. The times are simulated.
128 devices in a mesh: dp: 16 (over y_lo, x, core), tensor: 8 (over y_hi, z).
Axes of the slice: x: 4, y: 4 (y_hi: 2, y_lo: 2; y = y_hi * 2 + y_lo), z: 4, core: 2. Of those that a mesh axis runs over, the one named last changes fastest.
Arguments:
- tokens: bfloat16 [12288, 2048], P('dp'), may hold values from -6 to 6
- cotangent: bfloat16 [12288, 2048], P('dp'), may hold values from -6 to 6
- segments: int32 [12288], replicated, may hold values from 0 to 15, never falling along the last dimension, each value on 1 to 1537 neighbouring positions
- attn_norm_gain: float32 [2048], P('dp'), may hold values from 0.5 to 1.5
- attn_norm_bias: float32 [2048], P('dp'), may hold values from -1.25 to 1.25
- query_weight: float32 [2048, 2048], P('dp', 'tensor'), may hold values from -0.125 to 0.125
- query_bias: float32 [16, 128], P('tensor', 'dp'), may hold values from -1.25 to 1.25
- kv_weight: float32 [2048, 256], P('dp'), may hold values from -0.125 to 0.125
- value_bias: float32 [128], P('dp'), may hold values from -1.25 to 1.25
- out_weight: float32 [2048, 2048], P('tensor', 'dp'), may hold values from -0.5 to 0.5
- out_bias: float32 [2048], P('dp'), may hold values from -1.25 to 1.25
- mlp_norm_gain: float32 [2048], P('dp'), may hold values from 0.5 to 1.5
- mlp_norm_bias: float32 [2048], P('dp'), may hold values from -1.25 to 1.25
- up_weight: float32 [2048, 8192], P('dp', 'tensor'), may hold values from -0.125 to 0.125
- up_bias: float32 [64, 128], P('tensor', 'dp'), may hold values from -1.25 to 1.25
- down_weight: float32 [8192, 2048], P('tensor', 'dp'), may hold values from -0.0625 to 0.0625
- down_bias: float32 [2048], P('dp'), may hold values from -1.25 to 1.25
Outputs:
- output: bfloat16 [12288, 2048], P('dp')
- input_grad: float32 [12288, 2048], P('dp')
- attn_norm_gain_grad: float32 [2048], P('dp')
- attn_norm_bias_grad: float32 [2048], P('dp')
- query_weight_grad: float32 [2048, 2048], P('dp', 'tensor')
- query_bias_grad: float32 [16, 128], P('tensor', 'dp')
- kv_weight_grad: float32 [2048, 256], P('dp')
- value_bias_grad: float32 [128], P('dp')
- out_weight_grad: float32 [2048, 2048], P('tensor', 'dp')
- out_bias_grad: float32 [2048], P('dp')
- mlp_norm_gain_grad: float32 [2048], P('dp')
- mlp_norm_bias_grad: float32 [2048], P('dp')
- up_weight_grad: float32 [2048, 8192], P('dp', 'tensor')
- up_bias_grad: float32 [64, 128], P('tensor', 'dp')
- down_weight_grad: float32 [8192, 2048], P('tensor', 'dp')
- down_bias_grad: float32 [2048], P('dp')
Inputs may be any that keep to these rules, and one draw needn't show every extreme that they name: `segments`: segment numbers never fall along the stream; every document spans 1 to 1537 consecutive tokens, and some document spans exactly 1537.
All inputs are finite; a program needn't handle non-finite values.
Results may differ from a plain program's by a relative error of at most 0.03.
Values may be sent and summed in bfloat16 or wider, within the bound.
A program may use at most 192 MiB of HBM per device.

v0:
```python
import math
import jax
import jax.numpy as jnp
from jax import lax
from jax.sharding import PartitionSpec as P

HD = 128
DOC_MOST = 2000
EPS = 1e-05
NEG = -1e30


def from_behind(value, axis, steps):
    count = lax.axis_size(axis)
    initial, last = (max(0, -steps), min(count, count - steps))
    return lax.ppermute(value, axis, [(source, source + steps) for source in range(initial, last)])


def norm_rows(values, gain, shift):
    center = values - jnp.mean(values, axis=-1, keepdims=True)
    spread = jnp.mean(center * center, axis=-1, keepdims=True)
    return center * lax.rsqrt(spread + EPS) * gain + shift


def gelu_tanh(upward):
    inner = 0.7978845608028654 * (upward + 0.044715 * upward * upward * upward)
    return 0.5 * upward * (1.0 + jnp.tanh(inner))


def matmul(left, right):
    return jnp.dot(left, right, preferred_element_type=jnp.float32)


def contract_rows(left, right):
    return lax.dot_general(
        left, right, (((0,), (0,)), ((), ())), preferred_element_type=jnp.float32
    )


def contract_cols(left, right):
    return lax.dot_general(
        left, right, (((1,), (1,)), ((), ())), preferred_element_type=jnp.float32
    )


def heads_to_rows(matrix, local_heads, tok_rows):
    return (
        matrix.reshape(tok_rows, local_heads, HD)
        .transpose(1, 0, 2)
        .reshape(local_heads * tok_rows, HD)
    )


def rows_to_heads(matrix, local_heads, tok_rows):
    return (
        matrix.reshape(local_heads, tok_rows, HD)
        .transpose(1, 0, 2)
        .reshape(tok_rows, local_heads * HD)
    )


def body(
    tokens,
    cotangent,
    segments,
    attn_norm_gain,
    attn_norm_bias,
    query_weight,
    query_bias,
    kv_weight,
    value_bias,
    out_weight,
    out_bias,
    mlp_norm_gain,
    mlp_norm_bias,
    up_weight,
    up_bias,
    down_weight,
    down_bias,
):
    dp_size = lax.axis_size("dp")
    tok_rows = tokens.shape[0]
    local_heads = query_bias.shape[0]
    reach = min((DOC_MOST - 1) // tok_rows, dp_size // 2)
    window = (reach + 1) * tok_rows
    block_index = lax.axis_index("dp")
    scale = 1.0 / math.sqrt(HD)
    bf16 = jnp.bfloat16
    f32 = jnp.float32
    gathered = (
        lax.all_gather(attn_norm_gain.astype(bf16), "dp", axis=0, tiled=True),
        lax.all_gather(attn_norm_bias.astype(bf16), "dp", axis=0, tiled=True),
        lax.all_gather(query_weight.astype(bf16), "dp", axis=0, tiled=True),
        lax.all_gather(query_bias.astype(bf16), "dp", axis=1, tiled=True),
        lax.all_gather(kv_weight.astype(bf16), "dp", axis=0, tiled=True),
        lax.all_gather(value_bias.astype(bf16), "dp", axis=0, tiled=True),
        lax.all_gather(out_weight.astype(bf16), "dp", axis=1, tiled=True),
        lax.all_gather(out_bias.astype(bf16), "dp", axis=0, tiled=True),
        lax.all_gather(mlp_norm_gain.astype(bf16), "dp", axis=0, tiled=True),
        lax.all_gather(mlp_norm_bias.astype(bf16), "dp", axis=0, tiled=True),
        lax.all_gather(up_weight.astype(bf16), "dp", axis=0, tiled=True),
        lax.all_gather(up_bias.astype(bf16), "dp", axis=1, tiled=True),
        lax.all_gather(down_weight.astype(bf16), "dp", axis=1, tiled=True),
        lax.all_gather(down_bias.astype(bf16), "dp", axis=0, tiled=True),
    )
    gain_one = gathered[0].astype(f32)
    shift_one = gathered[1].astype(f32)
    query_w = gathered[2]
    query_b = gathered[3].reshape(-1).astype(f32)
    kv_w = gathered[4]
    value_b = gathered[5].astype(f32)
    out_w = gathered[6]
    out_b = gathered[7].astype(f32)
    gain_two = gathered[8].astype(f32)
    shift_two = gathered[9].astype(f32)
    up_w = gathered[10]
    up_b = gathered[11].reshape(-1).astype(f32)
    down_w = gathered[12]
    down_b = gathered[13].astype(f32)
    inputs = tokens.astype(f32)
    normed_one, norm_one_back = jax.vjp(norm_rows, inputs, gain_one, shift_one)
    normed_one = normed_one.astype(bf16)
    query = (matmul(normed_one, query_w) + query_b).astype(bf16)
    value_shift = jnp.concatenate([jnp.zeros((HD,), f32), value_b])
    keyval = (matmul(normed_one, kv_w) + value_shift).astype(bf16)
    pieces = []
    for offset in range(reach, 0, -1):
        pieces.append(from_behind(keyval, "dp", offset))
    window_kv = jnp.concatenate(pieces + [keyval], 0)
    window_keys = window_kv[:, :HD]
    window_values = window_kv[:, HD:]
    seg_padded = jnp.concatenate([jnp.full((reach * tok_rows,), -1, jnp.int32), segments])
    key_seg = lax.dynamic_slice_in_dim(seg_padded, block_index * tok_rows, window)
    query_seg = lax.dynamic_slice_in_dim(segments, block_index * tok_rows, tok_rows)
    key_place = jnp.arange(window, dtype=jnp.int32)
    query_place = reach * tok_rows + jnp.arange(tok_rows, dtype=jnp.int32)
    allowed = (query_seg[:, None] == key_seg[None, :]) & (
        key_place[None, :] <= query_place[:, None]
    )
    allowed = jnp.tile(allowed, (local_heads, 1))
    query_rows = heads_to_rows(query, local_heads, tok_rows)
    scores = jnp.where(allowed, contract_cols(query_rows, window_keys) * scale, NEG)
    top = jnp.max(scores, axis=-1, keepdims=True)
    log_total = top + jnp.log(jnp.sum(jnp.exp(scores - top), axis=-1, keepdims=True))
    probs = jnp.exp(scores - log_total).astype(bf16)
    attended = rows_to_heads(matmul(probs, window_values), local_heads, tok_rows).astype(bf16)
    middle = inputs + lax.psum(matmul(attended, out_w), "tensor") + out_b
    normed_two, norm_two_back = jax.vjp(norm_rows, middle, gain_two, shift_two)
    normed_two = normed_two.astype(bf16)
    hidden, gelu_back = jax.vjp(gelu_tanh, matmul(normed_two, up_w) + up_b)
    hidden = hidden.astype(bf16)
    output = (
        middle
        + lax.psum(matmul(hidden, down_w).astype(jnp.bfloat16), "tensor").astype(jnp.float32)
        + down_b
    ).astype(bf16)
    down_bias_grad = jnp.sum(cotangent.astype(f32), axis=0)
    down_weight_grad = contract_rows(hidden, cotangent)
    grad_hidden = contract_cols(cotangent, down_w)
    grad_up = gelu_back(grad_hidden)[0].astype(bf16)
    up_bias_grad = jnp.sum(grad_up.astype(f32), axis=0).reshape(-1, HD)
    up_weight_grad = contract_rows(normed_two, grad_up)
    grad_norm_two = lax.psum(contract_cols(grad_up, up_w), "tensor")
    grad_middle, mlp_gain_grad, mlp_shift_grad = norm_two_back(grad_norm_two)
    grad_middle = grad_middle + cotangent.astype(f32)
    grad_attn = grad_middle.astype(bf16)
    out_bias_grad = jnp.sum(grad_attn.astype(f32), axis=0)
    out_weight_grad = contract_rows(attended, grad_attn)
    grad_attended = contract_cols(grad_attn, out_w).astype(bf16)
    grad_rows = heads_to_rows(grad_attended, local_heads, tok_rows)
    scores_again = jnp.where(allowed, contract_cols(query_rows, window_keys) * scale, NEG)
    probs_again = jnp.exp(scores_again - log_total)
    grad_probs = contract_cols(grad_rows, window_values)
    delta = jnp.sum(probs_again * grad_probs, axis=-1, keepdims=True)
    grad_scores = (probs_again * (grad_probs - delta)).astype(bf16)
    grad_query = rows_to_heads(
        matmul(grad_scores, window_keys) * scale, local_heads, tok_rows
    ).astype(bf16)
    grad_keys = contract_rows(grad_scores, query_rows) * scale
    grad_values = contract_rows(probs_again.astype(bf16), grad_rows)
    grad_window = jnp.concatenate([grad_keys, grad_values], 1)
    own_kv_grad = grad_window[reach * tok_rows :]
    for offset in range(1, reach + 1):
        piece = grad_window[(reach - offset) * tok_rows : (reach - offset + 1) * tok_rows]
        own_kv_grad = own_kv_grad + from_behind(piece.astype(jnp.bfloat16), "dp", -offset).astype(
            piece.dtype
        )
    query_part = contract_cols(grad_query, query_w)
    grad_norm_query, kv_grad_total = (
        lax.psum(query_part.astype(jnp.bfloat16), "tensor").astype(jnp.float32),
        lax.psum(own_kv_grad.astype(jnp.bfloat16), "tensor").astype(jnp.float32),
    )
    kv_grad = kv_grad_total.astype(bf16)
    value_bias_grad = jnp.sum(kv_grad[:, HD:].astype(f32), axis=0)
    kv_weight_grad = contract_rows(normed_one, kv_grad)
    query_bias_grad = jnp.sum(grad_query.astype(f32), axis=0).reshape(local_heads, HD)
    query_weight_grad = contract_rows(normed_one, grad_query)
    grad_norm_one = grad_norm_query + contract_cols(kv_grad, kv_w)
    grad_inputs, attn_gain_grad, attn_shift_grad = norm_one_back(grad_norm_one)
    input_grad = grad_middle + grad_inputs
    summed = tuple(
        (
            lax.psum_scatter(
                attn_gain_grad.astype(jnp.bfloat16), "dp", scatter_dimension=0, tiled=True
            ).astype(jnp.float32),
            lax.psum_scatter(
                attn_shift_grad.astype(jnp.bfloat16), "dp", scatter_dimension=0, tiled=True
            ).astype(jnp.float32),
            lax.psum_scatter(
                query_weight_grad.astype(jnp.bfloat16), "dp", scatter_dimension=0, tiled=True
            ).astype(jnp.float32),
            lax.psum_scatter(
                query_bias_grad.astype(jnp.bfloat16), "dp", scatter_dimension=1, tiled=True
            ).astype(jnp.float32),
            lax.psum_scatter(
                kv_weight_grad.astype(jnp.bfloat16), "dp", scatter_dimension=0, tiled=True
            ).astype(jnp.float32),
            lax.psum_scatter(
                value_bias_grad.astype(jnp.bfloat16), "dp", scatter_dimension=0, tiled=True
            ).astype(jnp.float32),
            lax.psum_scatter(
                out_weight_grad.astype(jnp.bfloat16), "dp", scatter_dimension=1, tiled=True
            ).astype(jnp.float32),
            lax.psum_scatter(
                out_bias_grad.astype(jnp.bfloat16), "dp", scatter_dimension=0, tiled=True
            ).astype(jnp.float32),
            lax.psum_scatter(
                mlp_gain_grad.astype(jnp.bfloat16), "dp", scatter_dimension=0, tiled=True
            ).astype(jnp.float32),
            lax.psum_scatter(
                mlp_shift_grad.astype(jnp.bfloat16), "dp", scatter_dimension=0, tiled=True
            ).astype(jnp.float32),
            lax.psum_scatter(
                up_weight_grad.astype(jnp.bfloat16), "dp", scatter_dimension=0, tiled=True
            ).astype(jnp.float32),
            lax.psum_scatter(
                up_bias_grad.astype(jnp.bfloat16), "dp", scatter_dimension=1, tiled=True
            ).astype(jnp.float32),
            lax.psum_scatter(
                down_weight_grad.astype(jnp.bfloat16), "dp", scatter_dimension=1, tiled=True
            ).astype(jnp.float32),
            lax.psum_scatter(
                down_bias_grad.astype(jnp.bfloat16), "dp", scatter_dimension=0, tiled=True
            ).astype(jnp.float32),
        )
    )
    return (output, input_grad) + summed


def solution(mesh):
    return jax.shard_map(
        body,
        mesh=mesh,
        in_specs=(
            P("dp", None),
            P("dp", None),
            P(),
            P("dp"),
            P("dp"),
            P("dp", "tensor"),
            P("tensor", "dp"),
            P("dp", None),
            P("dp"),
            P("tensor", "dp"),
            P("dp"),
            P("dp"),
            P("dp"),
            P("dp", "tensor"),
            P("tensor", "dp"),
            P("tensor", "dp"),
            P("dp"),
        ),
        out_specs=(
            P("dp", None),
            P("dp", None),
            P("dp"),
            P("dp"),
            P("dp", "tensor"),
            P("tensor", "dp"),
            P("dp", None),
            P("dp"),
            P("tensor", "dp"),
            P("dp"),
            P("dp"),
            P("dp"),
            P("dp", "tensor"),
            P("tensor", "dp"),
            P("tensor", "dp"),
            P("dp"),
        ),
        check_vma=False,
    )
```

profile of v0, /device:TPU:0, one launch (start us, length us, event | category | flops | bytes accessed | tf_op | source)
XLA Modules:
  0.0 1073.2 jit_solution(2823137192838508573)
XLA Ops:
  16.5 30.5 %all-reduce.2 = bf16[128]{0:T(256)(128)(2,1)S(1)} all-reduce(bf16[128]{0:T(256)(128)(2,1)S(1)} %dynamic-update-slice), channel_id=1, replica_groups=mesh['dp'=16,'tensor'=8] {'dp'}, use_global_device_ids=true, to_apply=%add.2 | all-reduce | flops 128 | bytes 512
  50.4 15.9 %all-gather.1 = bf16[16,1,128]{2,1,0:T(2,128)(2,1)S(1)} all-gather(bf16[1,1,128]{2,1,0:T(2,128)(2,1)S(1)} %convert_bitcast_fusion.5), channel_id=1, replica_groups=mesh['dp'=16,'tensor'=8] {'dp'}, dimensions={0}, use_global_device_ids=true | all-gather | bytes 4352 | tf_op jit(solution)/shard_map/all_gather | solution.py:92
  66.3 17.8 %all-gather = bf16[16,1,128]{2,1,0:T(2,128)(2,1)S(1)} all-gather(bf16[1,1,128]{2,1,0:T(2,128)(2,1)S(1)} %convert_bitcast_fusion.6), channel_id=1, replica_groups=mesh['dp'=16,'tensor'=8] {'dp'}, dimensions={0}, use_global_device_ids=true | all-gather | bytes 4352 | tf_op jit(solution)/shard_map/all_gather | solution.py:91
  99.5 23.1 %all-gather.2 = bf16[16,8,2]{1,2,0:T(2,128)(2,1)S(1)} all-gather(bf16[1,8,2]{1,2,0:T(2,128)(2,1)S(1)} %convert_bitcast_fusion.4), channel_id=1, replica_groups=mesh['dp'=16,'tensor'=8] {'dp'}, dimensions={0}, use_global_device_ids=true | all-gather | bytes 544 | tf_op jit(solution)/shard_map/all_gather | solution.py:94
  132.4 6.7 fusion.54
  139.1 7.0 exponential_reduce_fusion
  146.1 9.8 fusion.1
  173.6 16.2 %all-gather.5 = bf16[16,1,128]{2,1,0:T(2,128)(2,1)S(1)} all-gather(bf16[1,1,128]{2,1,0:T(2,128)(2,1)S(1)} %convert_bitcast_fusion.1), channel_id=1, replica_groups=mesh['dp'=16,'tensor'=8] {'dp'}, dimensions={0}, use_global_device_ids=true | all-gather | bytes 4352 | tf_op jit(solution)/shard_map/all_gather | solution.py:100
  191.1 17.5 %all-gather.4 = bf16[16,1,128]{2,1,0:T(2,128)(2,1)S(1)} all-gather(bf16[1,1,128]{2,1,0:T(2,128)(2,1)S(1)} %convert_bitcast_fusion.2), channel_id=1, replica_groups=mesh['dp'=16,'tensor'=8] {'dp'}, dimensions={0}, use_global_device_ids=true | all-gather | bytes 4352 | tf_op jit(solution)/shard_map/all_gather | solution.py:99
  209.8 16.2 %all-gather.3 = bf16[16,1,128]{2,1,0:T(2,128)(2,1)S(1)} all-gather(bf16[1,1,128]{2,1,0:T(2,128)(2,1)S(1)} %convert_bitcast_fusion.3), channel_id=1, replica_groups=mesh['dp'=16,'tensor'=8] {'dp'}, dimensions={0}, use_global_device_ids=true | all-gather | bytes 4352 | tf_op jit(solution)/shard_map/all_gather | solution.py:98
  226.6 19.9 %all_gather.53 = bf16[8,128]{0,1:T(8,128)(2,1)} all-gather(bf16[8,8]{0,1:T(8,128)(2,1)} %copy.55), channel_id=1, replica_groups=mesh['dp'=16,'tensor'=8] {'dp'}, dimensions={1}, use_global_device_ids=true | all-gather | bytes 2176 | tf_op jit(solution)/shard_map/all_gather | solution.py:102
  249.1 65.9 %all-reduce.18.cloned.1.call-done = f32[768,2048]{1,0:T(8,128)} async-done(((f32[768,2048]{1,0:T(8,128)}), f32[768,2048]{1,0:T(8,128)}) %all-reduce.18.cloned.1.call-update) | async-done | bytes 6291472 | tf_op jit(solution)/shard_map/psum | solution.py:147
  323.4 28.4 %all-gather.19.cloned.1.call-done = bf16[2048,1024]{1,0:T(8,128)(2,1)} async-done(((bf16[128,1024]{1,0:T(8,128)(2,1)}), bf16[2048,1024]{1,0:T(8,128)(2,1)}) %all-gather.19.cloned.1.call-update) | async-done | bytes 4194320 | tf_op jit(solution)/shard_map/all_gather | solution.py:101
  351.7 9.2 fusion.43
  360.9 37.9 %all-gather.21.cloned.1.call-done = bf16[1024,2048]{1,0:T(8,128)(2,1)} async-done(((bf16[1024,128]{1,0:T(8,128)(2,1)}), bf16[1024,2048]{1,0:T(8,128)(2,1)}) %all-gather.21.cloned.1.call-update) | async-done | bytes 4194320 | tf_op jit(solution)/shard_map/all_gather | solution.py:103
  398.8 10.6 fusion.45
  416.2 8.7 convolution_convert_fusion
  424.9 6.5 copy.65
  431.5 131.4 %all-reduce.20.cloned.1.call-done = f32[768,2048]{1,0:T(8,128)} async-done(((f32[768,2048]{1,0:T(8,128)}), f32[768,2048]{1,0:T(8,128)}) %all-reduce.20.cloned.1.call-update) | async-done | bytes 6291472 | tf_op jit(solution)/shard_map/psum | solution.py:163
  562.9 6.5 multiply_reduce_fusion.1
  582.5 9.2 convolution_convert_fusion.1
  597.3 13.0 %multiply_reduce_fusion = (f32[1536]{0:T(1024)S(1)}, f32[1536,2304]{1,0:T(8,128)}) fusion(f32[1536,2304]{1,0:T(8,128)} %get-tuple-element.49, f32[1536]{0:T(1024)S(1)} %log_add_fusion, bf16[1536,128]{1,0:T(8,128)(2,1)S(1)} %bitcast.99, bf16[2304,256]{1,0:T(8,128)(2,1)} %copy-done.10), kind=kOutput, calls=%fused_computation.3 | convolution fusion | flops 916584960 | bytes 29306880 | tf_op jit(solution)/shard_map/dot_general | solution.py:41
  611.6 7.3 multiply_convert_fusion
  643.5 7.5 convolution_convert_fusion.3
  653.8 6.0 collective-permute-done.3
  662.1 17.5 %all-gather.6 = bf16[16,1,128]{2,1,0:T(2,128)(2,1)S(1)} all-gather(bf16[1,1,128]{2,1,0:T(2,128)(2,1)S(1)} %convert_bitcast_fusion), channel_id=1, replica_groups=mesh['dp'=16,'tensor'=8] {'dp'}, dimensions={0}, use_global_device_ids=true | all-gather | bytes 4352 | tf_op jit(solution)/shard_map/all_gather | solution.py:104
  682.2 9.6 reduce-scatter.18.cloned.1.call-done
  693.4 66.8 %reduce-scatter.16.cloned.1.call-done = bf16[128,1024]{1,0:T(8,128)(2,1)} async-done(((bf16[2048,1024]{1,0:T(8,128)(2,1)}), bf16[128,1024]{1,0:T(8,128)(2,1)}) %reduce-scatter.16.cloned.1.call-update) | async-done | bytes 262160 | tf_op jit(solution)/shard_map/reduce_scatter | solution.py:233
  762.0 60.6 %reduce-scatter.12.cloned.1.call-done = bf16[128,256]{1,0:T(8,128)(2,1)} async-done(((bf16[2048,256]{1,0:T(8,128)(2,1)}), bf16[128,256]{1,0:T(8,128)(2,1)}) %reduce-scatter.12.cloned.1.call-update) | async-done | bytes 65552 | tf_op jit(solution)/shard_map/reduce_scatter | solution.py:209
  824.1 154.3 %all-reduce.22.cloned.1.call-done = (bf16[768,2048]{1,0:T(8,128)(2,1)}, bf16[768,2048]{1,0:T(8,128)(2,1)}, bf16[768,256]{0,1:T(8,128)(2,1)}) async-done(((bf16[768,2048]{1,0:T(8,128)(2,1)}, bf16[768,2048]{1,0:T(8,128)(2,1)}, bf16[768,256]{0,1:T(8,128)(2,1)}), (bf16[768,2048]{1,0:T(8,128)(2,1)}, bf16[768,2048]{1,0:T(8,128)(2,1)}, bf16[768,256]{0,1:T(8,128)(2,1)})) %all-reduce.22.cloned.1.call-update) | async-done | bytes 6684688 | tf_op jit(solution)/shard_map/psum | solution.py:154
  991.1 55.5 %all-reduce.12 = (bf16[2048]{0:T(1024)(128)(2,1)S(1)}, bf16[2048]{0:T(1024)(128)(2,1)S(1)}, bf16[2,128]{1,0:T(2,128)(2,1)S(1)}, bf16[128]{0:T(256)(128)(2,1)S(1)...) all-reduce(bf16[2048]{0:T(1024)(128)(2,1)S(1)} %get-tuple-element.1, ...), channel_id=2, replica_groups=mesh['dp'=16,'tensor'=8] {'dp'}, use_global_device_ids=true, to_apply=%region_17.18.clone | all-reduce | flops 13696 | bytes 54784
  1050.3 6.8 add_convert_fusion
  (232 shorter events, 156.5 us)
Async XLA Ops:
  7.2 42.2 %copy-start.1 = (bf16[768,2048]{1,0:T(8,128)(2,1)S(1)}, bf16[768,2048]{1,0:T(8,128)(2,1)}, u32[]{:S(2)}) copy-start(bf16[768,2048]{1,0:T(8,128)(2,1)} %param.17) | copy-start | bytes 9437188
  7.2 76.9 %copy-start.25 = (s32[12288]{0:T(1024)S(1)}, s32[12288]{0:T(1024)}, u32[]{:S(2)}) copy-start(s32[12288]{0:T(1024)} %param.19) | copy-start | bytes 147460
  7.2 83.4 %all-gather.15.cloned.1.call-start = ((), (), s32[]{:S(2)}) async-start(), calls=%async_computation.6 | async-start | bytes 1114112 | tf_op jit(solution)/shard_map/all_gather | solution.py:95
  9.0 114.0 %all-gather.13.cloned.1.call-start = ((), (), s32[]{:S(2)}) async-start(), calls=%async_computation.5 | async-start | bytes 1114112 | tf_op jit(solution)/shard_map/all_gather | solution.py:93
  10.6 152.3 %all-gather.17.cloned.1.call-start = ((), (), s32[]{:S(2)}) async-start(), calls=%async_computation.7 | async-start | bytes 1114112 | tf_op jit(solution)/shard_map/all_gather | solution.py:97
  12.2 302.8 %all-reduce.18.cloned.1.call-start = ((), (), s32[]{:S(2)}) async-start(), calls=%async_computation.8 | async-start | bytes 12582912 | tf_op jit(solution)/shard_map/psum | solution.py:147
  49.4 38.3 %copy-start.18 = (f32[768]{0:T(1024)}, f32[768]{0:T(1024)S(1)}, u32[]{:S(2)}) copy-start(f32[768]{0:T(1024)S(1)} %broadcast_multiply_fusion.1) | copy-start | bytes 9220
  50.4 37.3 %copy-start.27 = (f32[768]{0:T(1024)}, f32[768]{0:T(1024)S(1)}, u32[]{:S(2)}) copy-start(f32[768]{0:T(1024)S(1)} %fusion.12) | copy-start | bytes 9220
  50.4 37.3 %copy-start.23 = (f32[768]{0:T(1024)}, f32[768]{0:T(1024)S(1)}, u32[]{:S(2)}) copy-start(f32[768]{0:T(1024)S(1)} %fusion.37) | copy-start | bytes 9220
  94.5 33.6 %collective-permute-start.1 = (bf16[768,256]{1,0:T(8,128)(2,1)}, bf16[768,256]{1,0:T(8,128)(2,1)}, u32[]{:S(2)}, u32[]{:S(2)}) collective-permute-start(bf16[768,256]{1,0:T(8,128)(2,1)} %fusion.27), channel_id=1, source_target_pairs={{0,8},{8,16},{16,24},{24,32},{32,40},{40,48},{48,56},{56,64},{64,7... | collective-permute-start | bytes 1179656 | tf_op jit(solution)/shard_map/ppermute | solution.py:16
  97.5 30.6 %collective-permute-start = (bf16[768,256]{1,0:T(8,128)(2,1)}, bf16[768,256]{1,0:T(8,128)(2,1)}, u32[]{:S(2)}, u32[]{:S(2)}) collective-permute-start(bf16[768,256]{1,0:T(8,128)(2,1)} %fusion.27), channel_id=1, source_target_pairs={{0,16},{8,24},{16,32},{24,40},{32,48},{40,56},{48,64},{56,72},{64,... | collective-permute-start | bytes 1179656 | tf_op jit(solution)/shard_map/ppermute | solution.py:16
  128.1 11.0 %copy-start.13 = (bf16[768,2,128]{2,0,1:T(8,128)(2,1)}, bf16[768,2,128]{2,0,1:T(8,128)(2,1)S(1)}, u32[]{:S(2)}) copy-start(bf16[768,2,128]{2,0,1:T(8,128)(2,1)S(1)} %copy.53) | copy-start | bytes 1179652
  129.6 9.5 copy-start.10
  167.9 183.9 %all-gather.19.cloned.1.call-start = ((), (), s32[]{:S(2)}) async-start(), calls=%async_computation.9 | async-start | bytes 4456448 | tf_op jit(solution)/shard_map/all_gather | solution.py:101
  169.7 229.1 %all-gather.21.cloned.1.call-start = ((), (), s32[]{:S(2)}) async-start(), calls=%async_computation.10 | async-start | bytes 4456448 | tf_op jit(solution)/shard_map/all_gather | solution.py:103
  171.6 391.3 %all-reduce.20.cloned.1.call-start = ((), (), s32[]{:S(2)}) async-start(), calls=%async_computation.11 | async-start | bytes 12582912 | tf_op jit(solution)/shard_map/psum | solution.py:163
  398.8 11.7 %copy-start.41 = (bf16[2048,1024]{1,0:T(8,128)(2,1)S(1)}, bf16[2048,1024]{1,0:T(8,128)(2,1)}, u32[]{:S(2)}) copy-start(bf16[2048,1024]{1,0:T(8,128)(2,1)} %all-gather.19.cloned.1.call-done) | copy-start | bytes 12582916
  415.9 264.3 %reduce-scatter.20.cloned.1.call-start = ((), (), s32[]{:S(2)}) async-start(), calls=%async_computation.16 | async-start | bytes 4456448
  431.4 260.3 %reduce-scatter.18.cloned.1.call-start = ((), (), s32[]{:S(2)}) async-start(), calls=%async_computation.15 | async-start | bytes 1114112
  582.5 177.7 %reduce-scatter.16.cloned.1.call-start = ((), (), s32[]{:S(2)}) async-start(), calls=%async_computation.14 | async-start | bytes 4456448 | tf_op jit(solution)/shard_map/reduce_scatter | solution.py:233
  591.7 230.8 %reduce-scatter.12.cloned.1.call-start = ((), (), s32[]{:S(2)}) async-start(), calls=%async_computation.12 | async-start | bytes 1114112 | tf_op jit(solution)/shard_map/reduce_scatter | solution.py:209
  597.2 13.1 %slice-start = ((s8[14155776]{0:T(1024)(128)(4,1)}), s8[4194304]{0:T(1024)(128)(4,1)S(1)}, s32[]{:S(2)}) async-start(s8[14155776]{0:T(1024)(128)(4,1)} %bitcast.92), calls=%async_computation.18 | async-start | bytes 8388608
  597.2 13.1 %slice-start.1 = ((s8[14155776]{0:T(1024)(128)(4,1)}), s8[4194304]{0:T(1024)(128)(4,1)S(1)}, s32[]{:S(2)}) async-start(s8[14155776]{0:T(1024)(128)(4,1)} %bitcast.92), calls=%async_computation.19 | async-start | bytes 8388608
  597.2 13.8 %slice-start.2 = ((s8[14155776]{0:T(1024)(128)(4,1)}), s8[4194304]{0:T(1024)(128)(4,1)S(1)}, s32[]{:S(2)}) async-start(s8[14155776]{0:T(1024)(128)(4,1)} %bitcast.92), calls=%async_computation.20 | async-start | bytes 8388608
  597.3 14.4 %slice-start.3 = ((s8[14155776]{0:T(1024)(128)(4,1)}), s8[1572864]{0:T(1024)(128)(4,1)S(1)}, s32[]{:S(2)}) async-start(s8[14155776]{0:T(1024)(128)(4,1)} %bitcast.92), calls=%async_computation.21 | async-start | bytes 3145728
  638.5 339.9 %all-reduce.22.cloned.1.call-start = ((), (), s32[]{:S(2)}) async-start(), calls=%async_computation.17 | async-start | bytes 13369344 | tf_op jit(solution)/shard_map/psum | solution.py:154
  640.5 13.3 %collective-permute-start.2 = (bf16[768,256]{0,1:T(8,128)(2,1)S(1)}, bf16[768,256]{0,1:T(8,128)(2,1)S(1)}, u32[]{:S(2)}, u32[]{:S(2)}) collective-permute-start(bf16[768,256]{0,1:T(8,128)(2,1)S(1)} %get-tuple-element.44), channel_id=1, source_target_pairs={{8,0},{16,8},{24,16},{32,24},{40,32},{48,40},{56,48},{64,56},{72,6... | collective-permute-start | bytes 1179656 | tf_op jit(solution)/shard_map/ppermute | solution.py:16
  641.8 9.2 copy-start.16
  641.8 17.9 %collective-permute-start.3 = (bf16[768,256]{0,1:T(8,128)(2,1)S(1)}, bf16[768,256]{0,1:T(8,128)(2,1)S(1)}, u32[]{:S(2)}, u32[]{:S(2)}) collective-permute-start(bf16[768,256]{0,1:T(8,128)(2,1)S(1)} %get-tuple-element.45), channel_id=1, source_target_pairs={{16,0},{24,8},{32,16},{40,24},{48,32},{56,40},{64,48},{72,56},{80,... | collective-permute-start | bytes 1179656 | tf_op jit(solution)/shard_map/ppermute | solution.py:16
  660.6 18.9 %copy-start.15 = (bf16[1536,128]{1,0:T(8,128)(2,1)S(1)}, bf16[1536,128]{1,0:T(8,128)(2,1)}, u32[]{:S(2)}) copy-start(bf16[1536,128]{1,0:T(8,128)(2,1)} %fusion.24) | copy-start | bytes 1179652
  660.7 404.0 %reduce-scatter.14.cloned.1.call-start = ((), (), s32[]{:S(2)}) async-start(), calls=%async_computation.13 | async-start | bytes 1114112 | tf_op jit(solution)/shard_map/reduce_scatter | solution.py:215
  762.0 221.4 %copy-start.19 = (f32[768]{0:T(1024)S(1)}, f32[768]{0:T(1024)}, u32[]{:S(2)}) copy-start(f32[768]{0:T(1024)} %copy-done.18) | copy-start | bytes 9220
  (36 other events, 175.7 us)
Sparse Core Ops, SparseCore 0:
  10.3 34.8 all-gather.14
  47.5 32.4 all-gather.12
  82.2 38.0 all-gather.16
  168.0 146.9 all-reduce.17
  317.2 34.5 all-gather.18
  353.8 44.9 all-gather.20
  416.1 146.8 all-reduce.19
  565.3 64.0 reduce-scatter.19
  631.8 59.9 reduce-scatter.17
  694.1 66.0 reduce-scatter.15
  762.7 59.8 reduce-scatter.11
  825.2 153.0 all-reduce.21
  983.5 58.6 reduce-scatter.13
where the time goes:
time: 1080 us; the launch traced here: 1070 us
  waiting for transfers between devices  561 us (52%)
  blocking collectives  230 us (21%)
  matrix products  124 us (11%)
  other arithmetic  99.1 us (9%)
  local copies, waits for them, and re-layouts  33.2 us (3%)
  between operations  17.2 us (2%)
    psum x1, waiting for transfers between devices, body(): lax.psum(matmul(hidden, down_w).astype(jnp.bfloat16), 'tensor')  154 us
    psum x1, waiting for transfers between devices, body(): grad_norm_two = lax.psum(contract_cols(grad_up, up_w), 'tensor')  131 us
    unnamed x2, blocking collectives  86 us
    reduce_scatter x1, waiting for transfers between devices, body(): lax.psum_scatter(up_weight_grad.astype(jnp.bfloat16), 'dp', scatter_dimen...  66.8 us
    psum x1, waiting for transfers between devices, body(): middle = inputs + lax.psum(matmul(attended, out_w), 'tensor') + out_b  65.9 us
    reduce_scatter x1, waiting for transfers between devices, body(): lax.psum_scatter(query_weight_grad.astype(jnp.bfloat16), 'dp', scatter_di...  60.6 us
    dot_general x7, matrix products, contract_cols(): lax.dot_general(left, right, (((1,), (1,)), ((), ())), preferred_element_...  47.1 us
    dot_general x7, matrix products, matmul(): return jnp.dot(left, right, preferred_element_type=jnp.float32)  38.4 us
  transfers between devices with their start and end apart: 17, of which 9 were waited for; matrix products, arithmetic and copies ran while one was open for 20% of the time, Pallas kernels for 0%

commit v1 on v0

--- a/solution.py
+++ b/solution.py
@@ -98,7 +98,10 @@
         lax.all_gather(out_bias.astype(bf16), "dp", axis=0, tiled=True),
         lax.all_gather(mlp_norm_gain.astype(bf16), "dp", axis=0, tiled=True),
         lax.all_gather(mlp_norm_bias.astype(bf16), "dp", axis=0, tiled=True),
-        lax.all_gather(up_weight.astype(bf16), "dp", axis=0, tiled=True),
+        jnp.concatenate(
+            lax.all_to_all(jnp.stack([up_weight.astype(bf16)] * lax.axis_size("dp")), "dp", 0, 0),
+            axis=0,
+        ),
         lax.all_gather(up_bias.astype(bf16), "dp", axis=1, tiled=True),
         lax.all_gather(down_weight.astype(bf16), "dp", axis=1, tiled=True),
         lax.all_gather(down_bias.astype(bf16), "dp", axis=0, tiled=True),

time: 1080 us -> 1090 us (level)
  waiting for transfers between devices: 561 us -> 511 us
  blocking collectives: 230 us -> 279 us
    all_gather x1, blocking collectives: 16.2 us -> 67.5 us  [body(): lax.all_gather(mlp_norm_bias.astype(bf16), 'dp', axis=0, tiled=True)]
    all_gather x1 -> x0, waiting for transfers between devices: 28.4 us -> none  [body(): lax.all_gather(up_weight.astype(bf16), 'dp', axis=0, tiled=True)]
    all_gather x1, waiting for transfers between devices: 37.9 us -> 26.6 us  [body(): lax.all_gather(down_weight.astype(bf16), 'dp', axis=1, tiled=True)]
    unnamed x110 -> x122, local copies, waits for them, and re-layouts: 23 us -> 22.4 us
  transfers between devices with their start and end apart: 17 -> 17, of which waited for: 9 -> 8; matrix products, arithmetic and copies ran while one was open for 20% -> 20% of each run, Pallas kernels for 0% -> 0%
where the time goes in v1:
time: 1090 us; the launch traced here: 1080 us
  waiting for transfers between devices  511 us (47%)
  blocking collectives  279 us (26%)
  matrix products  126 us (12%)
  other arithmetic  97.4 us (9%)
  local copies, waits for them, and re-layouts  35.1 us (3%)
  between operations  17.4 us (2%)
  starting transfers between devices  13.5 us (1%)
    psum x1, waiting for transfers between devices, body(): lax.psum(matmul(hidden, down_w).astype(jnp.bfloat16), 'tensor')  155 us
    psum x1, waiting for transfers between devices, body(): grad_norm_two = lax.psum(contract_cols(grad_up, up_w), 'tensor')  131 us
    unnamed x2, blocking collectives  85.5 us
    all_gather x1, blocking collectives, body(): lax.all_gather(mlp_norm_bias.astype(bf16), 'dp', axis=0, tiled=True)  67.5 us
    reduce_scatter x1, waiting for transfers between devices, body(): lax.psum_scatter(up_weight_grad.astype(jnp.bfloat16), 'dp', scatter_dimen...  67 us
    reduce_scatter x1, waiting for transfers between devices, body(): lax.psum_scatter(query_weight_grad.astype(jnp.bfloat16), 'dp', scatter_di...  60.5 us
    psum x1, waiting for transfers between devices, body(): middle = inputs + lax.psum(matmul(attended, out_w), 'tensor') + out_b  56.2 us
    dot_general x7, matrix products, contract_cols(): lax.dot_general(left, right, (((1,), (1,)), ((), ())), preferred_element_...  49.4 us
  transfers between devices with their start and end apart: 17, of which 8 were waited for; matrix products, arithmetic and copies ran while one was open for 20% of the time, Pallas kernels for 0%

profile of v1, /device:TPU:0, one launch (start us, length us, event | category | flops | bytes accessed | tf_op | source)
XLA Modules:
  0.0 1080.3 jit_solution(18031312033857163263)
XLA Ops:
  16.5 30.5 %all-reduce.2 = bf16[128]{0:T(256)(128)(2,1)S(1)} all-reduce(bf16[128]{0:T(256)(128)(2,1)S(1)} %dynamic-update-slice), channel_id=1, replica_groups=mesh['dp'=16,'tensor'=8] {'dp'}, use_global_device_ids=true, to_apply=%add.2 | all-reduce | flops 128 | bytes 512
  50.4 15.9 %all-gather.1 = bf16[16,1,128]{2,1,0:T(2,128)(2,1)S(1)} all-gather(bf16[1,1,128]{2,1,0:T(2,128)(2,1)S(1)} %convert_bitcast_fusion.5), channel_id=1, replica_groups=mesh['dp'=16,'tensor'=8] {'dp'}, dimensions={0}, use_global_device_ids=true | all-gather | bytes 4352 | tf_op jit(solution)/shard_map/all_gather | solution.py:92
  66.3 17.8 %all-gather = bf16[16,1,128]{2,1,0:T(2,128)(2,1)S(1)} all-gather(bf16[1,1,128]{2,1,0:T(2,128)(2,1)S(1)} %convert_bitcast_fusion.6), channel_id=1, replica_groups=mesh['dp'=16,'tensor'=8] {'dp'}, dimensions={0}, use_global_device_ids=true | all-gather | bytes 4352 | tf_op jit(solution)/shard_map/all_gather | solution.py:91
  99.5 23.1 %all-gather.2 = bf16[16,8,2]{1,2,0:T(2,128)(2,1)S(1)} all-gather(bf16[1,8,2]{1,2,0:T(2,128)(2,1)S(1)} %convert_bitcast_fusion.4), channel_id=1, replica_groups=mesh['dp'=16,'tensor'=8] {'dp'}, dimensions={0}, use_global_device_ids=true | all-gather | bytes 544 | tf_op jit(solution)/shard_map/all_gather | solution.py:94
  132.4 6.7 fusion.54
  139.1 7.0 exponential_reduce_fusion
  146.1 9.8 fusion.1
  178.7 67.5 %all-gather.5 = bf16[16,1,128]{2,1,0:T(2,128)(2,1)S(1)} all-gather(bf16[1,1,128]{2,1,0:T(2,128)(2,1)S(1)} %convert_bitcast_fusion.1), channel_id=1, replica_groups=mesh['dp'=16,'tensor'=8] {'dp'}, dimensions={0}, use_global_device_ids=true | all-gather | bytes 4352 | tf_op jit(solution)/shard_map/all_gather | solution.py:100
  247.5 16.5 %all-gather.4 = bf16[16,1,128]{2,1,0:T(2,128)(2,1)S(1)} all-gather(bf16[1,1,128]{2,1,0:T(2,128)(2,1)S(1)} %convert_bitcast_fusion.2), channel_id=1, replica_groups=mesh['dp'=16,'tensor'=8] {'dp'}, dimensions={0}, use_global_device_ids=true | all-gather | bytes 4352 | tf_op jit(solution)/shard_map/all_gather | solution.py:99
  264.7 17.5 %all-gather.3 = bf16[16,1,128]{2,1,0:T(2,128)(2,1)S(1)} all-gather(bf16[1,1,128]{2,1,0:T(2,128)(2,1)S(1)} %convert_bitcast_fusion.3), channel_id=1, replica_groups=mesh['dp'=16,'tensor'=8] {'dp'}, dimensions={0}, use_global_device_ids=true | all-gather | bytes 4352 | tf_op jit(solution)/shard_map/all_gather | solution.py:98
  282.8 18.0 %all_gather.49 = bf16[8,128]{0,1:T(8,128)(2,1)} all-gather(bf16[8,8]{0,1:T(8,128)(2,1)} %copy.55), channel_id=1, replica_groups=mesh['dp'=16,'tensor'=8] {'dp'}, dimensions={1}, use_global_device_ids=true | all-gather | bytes 2176 | tf_op jit(solution)/shard_map/all_gather | solution.py:105
  303.5 56.2 %all-reduce.18.cloned.1.call-done = f32[768,2048]{1,0:T(8,128)} async-done(((f32[768,2048]{1,0:T(8,128)}), f32[768,2048]{1,0:T(8,128)}) %all-reduce.18.cloned.1.call-update) | async-done | bytes 6291472 | tf_op jit(solution)/shard_map/psum | solution.py:150
  368.1 9.2 fusion.43
  377.3 26.6 %all-gather.18.cloned.1.call-done = bf16[1024,2048]{1,0:T(8,128)(2,1)} async-done(((bf16[1024,128]{1,0:T(8,128)(2,1)}), bf16[1024,2048]{1,0:T(8,128)(2,1)}) %all-gather.18.cloned.1.call-update) | async-done | bytes 4194320 | tf_op jit(solution)/shard_map/all_gather | solution.py:106
  403.9 10.4 fusion.45
  415.5 7.6 fusion.56
  423.3 8.7 convolution_convert_fusion
  432.0 6.6 copy.65
  438.6 131.4 %all-reduce.20.cloned.1.call-done = f32[768,2048]{1,0:T(8,128)} async-done(((f32[768,2048]{1,0:T(8,128)}), f32[768,2048]{1,0:T(8,128)}) %all-reduce.20.cloned.1.call-update) | async-done | bytes 6291472 | tf_op jit(solution)/shard_map/psum | solution.py:166
  570.0 6.5 multiply_reduce_fusion.1
  589.6 9.2 convolution_convert_fusion.1
  604.4 13.0 %multiply_reduce_fusion = (f32[1536]{0:T(1024)S(1)}, f32[1536,2304]{1,0:T(8,128)}) fusion(f32[1536,2304]{1,0:T(8,128)} %get-tuple-element.49, f32[1536]{0:T(1024)S(1)} %log_add_fusion, bf16[1536,128]{1,0:T(8,128)(2,1)S(1)} %bitcast.100, bf16[2304,256]{1,0:T(8,128)(2,1)} %copy-done.10), kind=kOutput, calls=%fused_computation.3 | convolution fusion | flops 916584960 | bytes 29306880 | tf_op jit(solution)/shard_map/dot_general | solution.py:41
  618.7 7.3 multiply_convert_fusion
  650.6 7.5 convolution_convert_fusion.3
  660.8 6.0 collective-permute-done.3
  669.2 17.5 %all-gather.6 = bf16[16,1,128]{2,1,0:T(2,128)(2,1)S(1)} all-gather(bf16[1,1,128]{2,1,0:T(2,128)(2,1)S(1)} %convert_bitcast_fusion), channel_id=1, replica_groups=mesh['dp'=16,'tensor'=8] {'dp'}, dimensions={0}, use_global_device_ids=true | all-gather | bytes 4352 | tf_op jit(solution)/shard_map/all_gather | solution.py:107
  689.9 9.0 reduce-scatter.18.cloned.1.call-done
  700.5 67.0 %reduce-scatter.16.cloned.1.call-done = bf16[128,1024]{1,0:T(8,128)(2,1)} async-done(((bf16[2048,1024]{1,0:T(8,128)(2,1)}), bf16[128,1024]{1,0:T(8,128)(2,1)}) %reduce-scatter.16.cloned.1.call-update) | async-done | bytes 262160 | tf_op jit(solution)/shard_map/reduce_scatter | solution.py:236
  769.3 60.5 %reduce-scatter.12.cloned.1.call-done = bf16[128,256]{1,0:T(8,128)(2,1)} async-done(((bf16[2048,256]{1,0:T(8,128)(2,1)}), bf16[128,256]{1,0:T(8,128)(2,1)}) %reduce-scatter.12.cloned.1.call-update) | async-done | bytes 65552 | tf_op jit(solution)/shard_map/reduce_scatter | solution.py:212
  831.3 154.5 %all-reduce.22.cloned.1.call-done = (bf16[768,2048]{1,0:T(8,128)(2,1)}, bf16[768,2048]{1,0:T(8,128)(2,1)}, bf16[768,256]{0,1:T(8,128)(2,1)}) async-done(((bf16[768,2048]{1,0:T(8,128)(2,1)}, bf16[768,2048]{1,0:T(8,128)(2,1)}, bf16[768,256]{0,1:T(8,128)(2,1)}), (bf16[768,2048]{1,0:T(8,128)(2,1)}, bf16[768,2048]{1,0:T(8,128)(2,1)}, bf16[768,256]{0,1:T(8,128)(2,1)})) %all-reduce.22.cloned.1.call-update) | async-done | bytes 6684688 | tf_op jit(solution)/shard_map/psum | solution.py:157
  998.6 54.9 %all-reduce.12 = (bf16[2048]{0:T(1024)(128)(2,1)S(1)}, bf16[2048]{0:T(1024)(128)(2,1)S(1)}, bf16[2,128]{1,0:T(2,128)(2,1)S(1)}, bf16[128]{0:T(256)(128)(2,1)S(1)...) all-reduce(bf16[2048]{0:T(1024)(128)(2,1)S(1)} %get-tuple-element.1, ...), channel_id=2, replica_groups=mesh['dp'=16,'tensor'=8] {'dp'}, use_global_device_ids=true, to_apply=%region_17.18.clone | all-reduce | flops 13696 | bytes 54784
  1057.2 6.8 add_convert_fusion
  (244 shorter events, 156.1 us)
Async XLA Ops:
  7.2 42.2 %copy-start.1 = (bf16[768,2048]{1,0:T(8,128)(2,1)S(1)}, bf16[768,2048]{1,0:T(8,128)(2,1)}, u32[]{:S(2)}) copy-start(bf16[768,2048]{1,0:T(8,128)(2,1)} %param.17) | copy-start | bytes 9437188
  7.2 76.9 %copy-start.27 = (s32[12288]{0:T(1024)S(1)}, s32[12288]{0:T(1024)}, u32[]{:S(2)}) copy-start(s32[12288]{0:T(1024)} %param.19) | copy-start | bytes 147460
  7.2 83.4 %all-gather.14.cloned.1.call-start = ((), (), s32[]{:S(2)}) async-start(), calls=%async_computation.7 | async-start | bytes 1114112 | tf_op jit(solution)/shard_map/all_gather | solution.py:95
  9.0 114.0 %all-gather.12.cloned.1.call-start = ((), (), s32[]{:S(2)}) async-start(), calls=%async_computation.6 | async-start | bytes 1114112 | tf_op jit(solution)/shard_map/all_gather | solution.py:93
  10.6 152.3 %all-gather.16.cloned.1.call-start = ((), (), s32[]{:S(2)}) async-start(), calls=%async_computation.8 | async-start | bytes 1114112 | tf_op jit(solution)/shard_map/all_gather | solution.py:97
  12.2 347.6 %all-reduce.18.cloned.1.call-start = ((), (), s32[]{:S(2)}) async-start(), calls=%async_computation.9 | async-start | bytes 12582912 | tf_op jit(solution)/shard_map/psum | solution.py:150
  49.4 38.3 %copy-start.20 = (f32[768]{0:T(1024)}, f32[768]{0:T(1024)S(1)}, u32[]{:S(2)}) copy-start(f32[768]{0:T(1024)S(1)} %broadcast_multiply_fusion.1) | copy-start | bytes 9220
  50.4 37.3 %copy-start.29 = (f32[768]{0:T(1024)}, f32[768]{0:T(1024)S(1)}, u32[]{:S(2)}) copy-start(f32[768]{0:T(1024)S(1)} %fusion.12) | copy-start | bytes 9220
  50.4 37.3 %copy-start.25 = (f32[768]{0:T(1024)}, f32[768]{0:T(1024)S(1)}, u32[]{:S(2)}) copy-start(f32[768]{0:T(1024)S(1)} %fusion.37) | copy-start | bytes 9220
  94.6 33.5 %collective-permute-start.1 = (bf16[768,256]{1,0:T(8,128)(2,1)}, bf16[768,256]{1,0:T(8,128)(2,1)}, u32[]{:S(2)}, u32[]{:S(2)}) collective-permute-start(bf16[768,256]{1,0:T(8,128)(2,1)} %fusion.27), channel_id=1, source_target_pairs={{0,8},{8,16},{16,24},{24,32},{32,40},{40,48},{48,56},{56,64},{64,7... | collective-permute-start | bytes 1179656 | tf_op jit(solution)/shard_map/ppermute | solution.py:16
  97.5 30.6 %collective-permute-start = (bf16[768,256]{1,0:T(8,128)(2,1)}, bf16[768,256]{1,0:T(8,128)(2,1)}, u32[]{:S(2)}, u32[]{:S(2)}) collective-permute-start(bf16[768,256]{1,0:T(8,128)(2,1)} %fusion.27), channel_id=1, source_target_pairs={{0,16},{8,24},{16,32},{24,40},{32,48},{40,56},{48,64},{56,72},{64,... | collective-permute-start | bytes 1179656 | tf_op jit(solution)/shard_map/ppermute | solution.py:16
  128.1 11.0 %copy-start.13 = (bf16[768,2,128]{2,0,1:T(8,128)(2,1)}, bf16[768,2,128]{2,0,1:T(8,128)(2,1)S(1)}, u32[]{:S(2)}) copy-start(bf16[768,2,128]{2,0,1:T(8,128)(2,1)S(1)} %copy.53) | copy-start | bytes 1179652
  129.6 9.5 copy-start.10
  167.9 236.0 %all-gather.18.cloned.1.call-start = ((), (), s32[]{:S(2)}) async-start(), calls=%async_computation.10 | async-start | bytes 4456448 | tf_op jit(solution)/shard_map/all_gather | solution.py:106
  173.3 194.8 %all-to-all-start = ((bf16[16,128,1024]{2,1,0:T(8,128)(2,1)}), bf16[16,128,1024]{2,1,0:T(8,128)(2,1)}, u32[]{:S(2)}, u32[]{:S(2)}) async-start(bf16[16,128,1024]{2,1,0:T(8,128)(2,1)} %stack.2), calls=%async_computation | async-start | bytes 8388608 | tf_op jit(solution)/shard_map/all_to_all | solution.py:102
  178.0 392.0 %all-reduce.20.cloned.1.call-start = ((), (), s32[]{:S(2)}) async-start(), calls=%async_computation.11 | async-start | bytes 12582912 | tf_op jit(solution)/shard_map/psum | solution.py:166
  423.1 264.9 %reduce-scatter.20.cloned.1.call-start = ((), (), s32[]{:S(2)}) async-start(), calls=%async_computation.16 | async-start | bytes 4456448
  438.6 260.3 %reduce-scatter.18.cloned.1.call-start = ((), (), s32[]{:S(2)}) async-start(), calls=%async_computation.15 | async-start | bytes 1114112
  589.6 177.9 %reduce-scatter.16.cloned.1.call-start = ((), (), s32[]{:S(2)}) async-start(), calls=%async_computation.14 | async-start | bytes 4456448 | tf_op jit(solution)/shard_map/reduce_scatter | solution.py:236
  598.8 231.0 %reduce-scatter.12.cloned.1.call-start = ((), (), s32[]{:S(2)}) async-start(), calls=%async_computation.12 | async-start | bytes 1114112 | tf_op jit(solution)/shard_map/reduce_scatter | solution.py:212
  604.3 13.1 %slice-start = ((s8[14155776]{0:T(1024)(128)(4,1)}), s8[4194304]{0:T(1024)(128)(4,1)S(1)}, s32[]{:S(2)}) async-start(s8[14155776]{0:T(1024)(128)(4,1)} %bitcast.93), calls=%async_computation.18 | async-start | bytes 8388608
  604.3 13.1 %slice-start.1 = ((s8[14155776]{0:T(1024)(128)(4,1)}), s8[4194304]{0:T(1024)(128)(4,1)S(1)}, s32[]{:S(2)}) async-start(s8[14155776]{0:T(1024)(128)(4,1)} %bitcast.93), calls=%async_computation.19 | async-start | bytes 8388608
  604.3 13.8 %slice-start.2 = ((s8[14155776]{0:T(1024)(128)(4,1)}), s8[4194304]{0:T(1024)(128)(4,1)S(1)}, s32[]{:S(2)}) async-start(s8[14155776]{0:T(1024)(128)(4,1)} %bitcast.93), calls=%async_computation.20 | async-start | bytes 8388608
  604.3 14.4 %slice-start.3 = ((s8[14155776]{0:T(1024)(128)(4,1)}), s8[1572864]{0:T(1024)(128)(4,1)S(1)}, s32[]{:S(2)}) async-start(s8[14155776]{0:T(1024)(128)(4,1)} %bitcast.93), calls=%async_computation.21 | async-start | bytes 3145728
  645.5 340.3 %all-reduce.22.cloned.1.call-start = ((), (), s32[]{:S(2)}) async-start(), calls=%async_computation.17 | async-start | bytes 13369344 | tf_op jit(solution)/shard_map/psum | solution.py:157
  647.6 13.2 %collective-permute-start.2 = (bf16[768,256]{0,1:T(8,128)(2,1)S(1)}, bf16[768,256]{0,1:T(8,128)(2,1)S(1)}, u32[]{:S(2)}, u32[]{:S(2)}) collective-permute-start(bf16[768,256]{0,1:T(8,128)(2,1)S(1)} %get-tuple-element.44), channel_id=1, source_target_pairs={{8,0},{16,8},{24,16},{32,24},{40,32},{48,40},{56,48},{64,56},{72,6... | collective-permute-start | bytes 1179656 | tf_op jit(solution)/shard_map/ppermute | solution.py:16
  648.9 17.9 %collective-permute-start.3 = (bf16[768,256]{0,1:T(8,128)(2,1)S(1)}, bf16[768,256]{0,1:T(8,128)(2,1)S(1)}, u32[]{:S(2)}, u32[]{:S(2)}) collective-permute-start(bf16[768,256]{0,1:T(8,128)(2,1)S(1)} %get-tuple-element.45), channel_id=1, source_target_pairs={{16,0},{24,8},{32,16},{40,24},{48,32},{56,40},{64,48},{72,56},{80,... | collective-permute-start | bytes 1179656 | tf_op jit(solution)/shard_map/ppermute | solution.py:16
  667.7 19.5 %copy-start.15 = (bf16[1536,128]{1,0:T(8,128)(2,1)S(1)}, bf16[1536,128]{1,0:T(8,128)(2,1)}, u32[]{:S(2)}) copy-start(bf16[1536,128]{1,0:T(8,128)(2,1)} %fusion.24) | copy-start | bytes 1179652
  667.8 403.8 %reduce-scatter.14.cloned.1.call-start = ((), (), s32[]{:S(2)}) async-start(), calls=%async_computation.13 | async-start | bytes 1114112 | tf_op jit(solution)/shard_map/reduce_scatter | solution.py:218
  769.3 221.2 %copy-start.19 = (f32[16,1,128]{2,1,0:T(1,128)S(1)}, f32[16,1,128]{2,1,0:T(1,128)}, u32[]{:S(2)}) copy-start(f32[16,1,128]{2,1,0:T(1,128)} %copy-done.18) | copy-start | bytes 24580
  769.3 221.2 %copy-start.21 = (f32[768]{0:T(1024)S(1)}, f32[768]{0:T(1024)}, u32[]{:S(2)}) copy-start(f32[768]{0:T(1024)} %copy-done.20) | copy-start | bytes 9220
  995.6 61.6 %copy-start.35 = (f32[16,1,128]{2,1,0:T(1,128)S(1)}, f32[16,1,128]{2,1,0:T(1,128)}, u32[]{:S(2)}) copy-start(f32[16,1,128]{2,1,0:T(1,128)} %convert_element_type.339) | copy-start | bytes 24580
  (42 other events, 202.9 us)
Sparse Core Ops, SparseCore 0:
  10.3 34.8 all-gather.13
  47.5 32.4 all-gather.11
  82.2 38.0 all-gather.15
  168.0 191.6 all-reduce.17
  361.8 42.0 all-gather.17
  423.2 146.8 all-reduce.19
  572.4 64.0 reduce-scatter.19
  638.9 59.9 reduce-scatter.17
  701.4 66.0 reduce-scatter.15
  769.8 59.9 reduce-scatter.11
  832.6 153.2 all-reduce.21
  990.6 58.5 reduce-scatter.13
